TPU v7x, 128 devices: a whole 4x4x4 slice. The times are simulated.
128 devices in a mesh: tm: 2 (over core), rows: 64 (over z, x, y).
Axes of the slice: x: 4, y: 4, z: 4, core: 2. Of those that a mesh axis runs over, the one named last changes fastest.
Arguments:
- feat: bfloat16 [4, 128, 240, 512], P('tm', 'rows'), may hold values from -24 to 24
- norm1_gain: float32 [512], replicated, may hold values from 0.5 to 1.5
- norm1_bias: float32 [512], replicated, may hold values from -3 to 3
- conv_weight: bfloat16 [3, 3, 3, 512, 512], replicated, may hold values from -0.0546875 to 0.0546875
- conv_bias: float32 [512], replicated, may hold values from -3 to 3
- norm2_gain: float32 [512], replicated, may hold values from 0.5 to 1.5
- norm2_bias: float32 [512], replicated, may hold values from -3 to 3
- w_query: bfloat16 [512, 512], replicated, may hold values from -0.44194174 to 0.44194174
- w_key: bfloat16 [512, 512], replicated, may hold values from -1.5467961 to 1.5467961
- w_value: bfloat16 [512, 512], replicated, may hold values from -0.25 to 0.25
- w_out: bfloat16 [512, 512], replicated, may hold values from -0.25 to 0.25
- out_bias: float32 [512], replicated, may hold values from -3 to 3
Outputs:
- block_out: bfloat16 [4, 128, 240, 512], P('tm', 'rows')
All inputs are finite; a program needn't handle non-finite values.
Results may differ from a plain program's by a relative error of at most 0.0062.
The roundings to bfloat16 on the way count: a program that leaves them out, or rounds other values in their place, can miss the bound.
Values may be sent and summed in bfloat16 or wider, within the bound.
No kernel may reach another device: no remote copies, remote signals or barrier semaphores. Data moves between devices by JAX's collectives and lax.ppermute only.
A program may use at most 128 MiB of HBM per device.

v0:
```python
import math
import jax
import jax.numpy as jnp
from jax import lax
from jax.sharding import PartitionSpec as P

GROUPS = 32
RADIUS = 4
EPS = 1e-06


def from_behind(array, axis, by):
    peers = lax.axis_size(axis)
    pairs = [(i, i + by) for i in range(peers) if 0 <= i + by < peers]
    return lax.ppermute(array, axis, pairs)


def padded_2(cells, sides, width):
    for axis, dim in sides:
        count = lax.axis_size(axis)
        ends = count - 1
        head = lax.slice_in_dim(cells, 0, width, axis=dim)
        tail = lax.slice_in_dim(cells, cells.shape[dim] - width, cells.shape[dim], axis=dim)
        cells = jnp.concatenate(
            [
                lax.ppermute(tail, axis, [(i, (i + 1) % count) for i in range(ends)]),
                cells,
                lax.ppermute(head, axis, [((i + 1) % count, i) for i in range(ends)]),
            ],
            axis=dim,
        )
    return cells


def group_norm(values, gain, shift, count):
    chans = values.shape[-1]
    grouped = values.reshape(values.shape[:-1] + (GROUPS, chans // GROUPS))
    local_sum = jnp.sum(grouped, axis=(0, 1, 2, 4))
    mean = lax.psum(local_sum, ("tm", "rows")) / count
    centered = grouped - mean[:, None]
    spread = lax.psum(jnp.sum(centered * centered, axis=(0, 1, 2, 4)), ("tm", "rows")) / count
    normed = centered * lax.rsqrt(spread + EPS)[:, None]
    return normed.reshape(values.shape) * gain + shift


def conv_taps(padded, weight, frames, height, width):
    chans = padded.shape[-1]
    total = jnp.zeros((frames * height * width, weight.shape[-1]), jnp.float32)
    for step_t in range(3):
        for step_h in range(3):
            slab = padded[step_t : step_t + frames, step_h : step_h + height]
            stacked = jnp.concatenate(
                [slab[:, :, step_w : step_w + width] for step_w in range(3)], axis=-1
            )
            total = total + jnp.dot(
                stacked.reshape(-1, 3 * chans),
                weight[step_t, step_h].reshape(3 * chans, -1),
                preferred_element_type=jnp.float32,
            )
    return total.reshape(frames, height, width, -1)


def project(flat, weight):
    return jnp.dot(flat, weight, preferred_element_type=jnp.float32).astype(jnp.bfloat16)


def shards(
    feat,
    norm1_gain,
    norm1_bias,
    conv_weight,
    conv_bias,
    norm2_gain,
    norm2_bias,
    w_query,
    w_key,
    w_value,
    w_out,
    out_bias,
):
    frames, stripe_rows, width, chans = feat.shape
    stripes = lax.axis_size("rows")
    count = lax.axis_size("tm") * stripes * frames * stripe_rows * width * (chans // GROUPS)
    act = jax.nn.silu(group_norm(feat.astype(jnp.float32), norm1_gain, norm1_bias, count)).astype(
        jnp.bfloat16
    )
    earlier = from_behind(act, "tm", 1)
    opening = jnp.broadcast_to(act[:1], earlier.shape)
    earlier = jnp.where(lax.axis_index("tm") == 0, opening, earlier)
    timed = jnp.concatenate([earlier, act], axis=0)
    rimmed = padded_2(timed, (("rows", 1),), 1)
    padded = jnp.pad(rimmed, ((0, 0), (0, 0), (1, 1), (0, 0)))
    conv = conv_taps(padded, conv_weight, frames, stripe_rows, width) + conv_bias
    resid = (feat.astype(jnp.float32) + conv).astype(jnp.bfloat16)
    normed = group_norm(resid.astype(jnp.float32), norm2_gain, norm2_bias, count).astype(
        jnp.bfloat16
    )
    flat = normed.reshape(-1, chans)
    query = project(flat, w_query).reshape(frames, -1, chans)
    reach = RADIUS * stripe_rows
    paired = jnp.stack([project(flat, w_key), project(flat, w_value)]).reshape(
        2, frames, stripe_rows, width, chans
    )
    pieces = []
    for offset in range(-RADIUS, RADIUS + 1):
        if offset == 0:
            pieces.append(paired)
        else:
            pieces.append(from_behind(paired, "rows", -offset))
    wide = jnp.concatenate(pieces, axis=2)
    keys = wide[0].reshape(frames, -1, chans)
    values = wide[1].reshape(frames, -1, chans)
    span = 2 * reach + stripe_rows
    place = lax.axis_index("rows") * stripe_rows - reach + jnp.arange(span, dtype=jnp.int32)
    valid = jnp.repeat((place >= 0) & (place < stripes * stripe_rows), width)
    scale = 1.0 / math.sqrt(chans)
    scores = jnp.einsum("fqc,fkc->fqk", query, keys, preferred_element_type=jnp.float32) * scale
    scores = jnp.where(valid[None, None, :], scores, jnp.float32(-1e30))
    top = jnp.max(scores, axis=-1, keepdims=True)
    expo = jnp.exp(scores - top)
    total = jnp.sum(expo, axis=-1, keepdims=True)
    mixed = jnp.einsum(
        "fqk,fkc->fqc", expo.astype(jnp.bfloat16), values, preferred_element_type=jnp.float32
    )
    attn = (mixed / total).astype(jnp.bfloat16).reshape(-1, chans)
    output = jnp.dot(attn, w_out, preferred_element_type=jnp.float32).reshape(
        frames, stripe_rows, width, chans
    )
    return (resid.astype(jnp.float32) + out_bias + output).astype(jnp.bfloat16)


def solution(mesh):
    return jax.shard_map(
        shards,
        mesh=mesh,
        in_specs=(
            P("tm", "rows", None, None),
            P(),
            P(),
            P(),
            P(),
            P(),
            P(),
            P(),
            P(),
            P(),
            P(),
            P(),
        ),
        out_specs=P("tm", "rows", None, None),
        check_vma=False,
    )
```

profile of v0, /device:TPU:54, one launch (start us, length us, event | category | flops | bytes accessed | tf_op | source)
XLA Modules:
  0.0 680.6 jit_solution(8682278299150185639)
XLA Ops:
  1.7 63.7 %psum.28 = f32[32]{0:T(128)S(1)} all-reduce(f32[32]{0:T(128)S(1)} %reduce_sum.59), channel_id=1, replica_groups=mesh['tm'=2,'rows'=64] {'tm','rows'}, use_global_device_ids=true, to_apply=%region_2.0 | all-reduce | flops 32 | bytes 256 | tf_op jit(solution)/shard_map/psum | solution.py:39
  67.2 63.0 %psum.29 = f32[32]{0:T(128)S(1)} all-reduce(f32[32]{0:T(128)S(1)} %reduce_sum.62), channel_id=1, replica_groups=mesh['tm'=2,'rows'=64] {'tm','rows'}, use_global_device_ids=true, to_apply=%region_5.6 | all-reduce | flops 32 | bytes 256 | tf_op jit(solution)/shard_map/psum | solution.py:41
  136.5 3.7 collective-permute-start.1
  142.5 9.3 %fusion.44 = (bf16[1,1,3,512,512]{4,3,2,1,0:T(8,128)(2,1)S(1)}, bf16[1,1,3,512,512]{4,3,2,1,0:T(8,128)(2,1)}, bf16[1,1,3,512,512]{4,3,2,1,0:T(8,128)(2,1)}, bf16...) fusion(bf16[3,3,3,512,512]{4,3,2,1,0:T(8,128)(2,1)} %param.15), kind=kLoop, calls=%fused_computation.89 | loop fusion | bytes 28311552 | tf_op jit(solution)/shard_map/slice | solution.py:57
  151.8 10.6 %collective-permute-done.1 = bf16[4,1,240,512]{3,2,1,0:T(8,128)(2,1)S(1)} collective-permute-done((bf16[4,1,240,512]{3,2,1,0:T(8,128)(2,1)S(1)}, bf16[4,1,240,512]{3,2,1,0:T(8,128)(2,1)S(1)}, u32[]{:S(2)}, u32[]{:S(2)}) %collective-permute-start.1) | collective-permute-done | bytes 983072 | tf_op jit(solution)/shard_map/ppermute | solution.py:26
  162.4 4.4 collective-permute-done.2
  168.8 6.3 fusion.45
  200.8 66.5 %psum.30 = f32[32]{0:T(128)S(1)} all-reduce(f32[32]{0:T(128)S(1)} %reduce_sum.81), channel_id=1, replica_groups=mesh['tm'=2,'rows'=64] {'tm','rows'}, use_global_device_ids=true, to_apply=%region_8.9 | all-reduce | flops 32 | bytes 256 | tf_op jit(solution)/shard_map/psum | solution.py:39
  268.0 64.1 %psum.31 = f32[32]{0:T(128)S(1)} all-reduce(f32[32]{0:T(128)S(1)} %reduce_sum.84), channel_id=1, replica_groups=mesh['tm'=2,'rows'=64] {'tm','rows'}, use_global_device_ids=true, to_apply=%region_11.12 | all-reduce | flops 32 | bytes 256 | tf_op jit(solution)/shard_map/psum | solution.py:41
  336.6 3.8 collective-permute-start.3
  340.4 3.2 collective-permute-start.4
  343.6 4.6 collective-permute-start.5
  348.2 3.0 collective-permute-start.6
  351.2 2.8 collective-permute-start.7
  354.1 30.5 %collective-permute-done.3 = bf16[2,2,2,240,512]{4,3,2,1,0:T(8,128)(2,1)} collective-permute-done((bf16[2,2,2,240,512]{4,3,2,1,0:T(8,128)(2,1)}, bf16[2,2,2,240,512]{4,3,2,1,0:T(8,128)(2,1)}, u32[]{:S(2)}, u32[]{:S(2)}) %collective-permute-start.3) | collective-permute-done | bytes 1966112 | tf_op jit(solution)/shard_map/ppermute | solution.py:15
  387.1 39.4 %collective-permute-done.4 = bf16[2,2,2,240,512]{4,3,2,1,0:T(8,128)(2,1)} collective-permute-done((bf16[2,2,2,240,512]{4,3,2,1,0:T(8,128)(2,1)}, bf16[2,2,2,240,512]{4,3,2,1,0:T(8,128)(2,1)}, u32[]{:S(2)}, u32[]{:S(2)}) %collective-permute-start.4) | collective-permute-done | bytes 1966112 | tf_op jit(solution)/shard_map/ppermute | solution.py:15
  426.5 90.0 %collective-permute-start.9 = (bf16[2,2,2,240,512]{4,3,2,1,0:T(8,128)(2,1)}, bf16[2,2,2,240,512]{4,3,2,1,0:T(8,128)(2,1)}, u32[]{:S(2)}, u32[]{:S(2)}) collective-permute-start(bf16[2,2,2,240,512]{4,3,2,1,0:T(8,128)(2,1)} %pad_maximum_fusion.10), channel_id=1, source_target_pairs={{3,0},{4,1},{5,2},{6,3},{7,4},{8,5},{9,6},{10,7},{11,8},{12,9},{13... | collective-permute-start | bytes 5898248 | tf_op jit(solution)/shard_map/ppermute | solution.py:15
  516.5 3.1 collective-permute-start.10
  532.8 27.3 %collective-permute-done.9 = bf16[2,2,2,240,512]{4,3,2,1,0:T(8,128)(2,1)} collective-permute-done((bf16[2,2,2,240,512]{4,3,2,1,0:T(8,128)(2,1)}, bf16[2,2,2,240,512]{4,3,2,1,0:T(8,128)(2,1)}, u32[]{:S(2)}, u32[]{:S(2)}) %collective-permute-start.9) | collective-permute-done | bytes 1966112 | tf_op jit(solution)/shard_map/ppermute | solution.py:15
  561.7 80.5 %collective-permute-done.10 = bf16[2,2,2,240,512]{4,3,2,1,0:T(8,128)(2,1)} collective-permute-done((bf16[2,2,2,240,512]{4,3,2,1,0:T(8,128)(2,1)}, bf16[2,2,2,240,512]{4,3,2,1,0:T(8,128)(2,1)}, u32[]{:S(2)}, u32[]{:S(2)}) %collective-permute-start.10) | collective-permute-done | bytes 1966112 | tf_op jit(solution)/shard_map/ppermute | solution.py:15
  643.9 4.3 fusion.43
  648.2 10.2 %fusion = (f32[2,480]{1,0:T(2,128)S(1)}, f32[2,480,4320]{2,1,0:T(8,128)}) fusion(pred[4320]{0:T(1024)(128)(4,1)S(1)} %broadcast_in_dim.35, bf16[2,480,512]{2,1,0:T(8,128)(2,1)} %bitcast.89, bf16[2,4320,512]{2,1,0:T(8,128)(2,1)S(1)} %bitcast.63), kind=kOutput, calls=%fused_computation.2 | convolution fusion | flops 4259173376 | bytes 26427360 | tf_op jit(solution)/shard_map/fqc,fkc->fqk/dot_general | solution.py:117
  658.4 9.5 %fusion.1 = f32[2,480]{1,0:T(2,128)S(1)} fusion(f32[2,480,4320]{2,1,0:T(8,128)} %get-tuple-element.50, f32[2,480]{1,0:T(2,128)S(1)} %get-tuple-element.49, pred[4320]{0:T(1024)(128)(4,1)S(1)} %broadcast_in_dim.35), kind=kLoop, calls=%fused_computation.3 | loop fusion | flops 16587840 | bytes 16600800 | tf_op jit(solution)/shard_map/reduce_sum | solution.py:121
  667.9 11.0 %divide_convert_fusion = bf16[2,480,512]{2,1,0:T(8,128)(2,1)S(1)} fusion(bf16[2,4320,512]{2,1,0:T(8,128)(2,1)} %bitcast.62, f32[2,480,4320]{2,1,0:T(8,128)} %get-tuple-element.50, f32[2,480]{1,0:T(2,128)S(1)} %get-tuple-element.49, pred[4320]{0:T(1024)(128)(4,1)S(1)} %broadcast_in_dim.35, f32[2,480]{1,0:T(2,128)S(1)} %fusion.1), kind=kOutput, calls=%fused_computation.62 | convolution fusion | flops 4264304640 | bytes 26431200 | tf_op jit(solution)/shard_map/fqk,fkc->fqc/dot_general | solution.py:122
  (129 shorter events, 65.3 us)
Async XLA Ops:
  0.0 332.7 %copy-start = (bf16[512,512]{1,0:T(8,128)(2,1)S(1)}, bf16[512,512]{1,0:T(8,128)(2,1)}, u32[]{:S(2)}) copy-start(bf16[512,512]{1,0:T(8,128)(2,1)} %param.20) | copy-start | bytes 1572868
  132.3 3.9 collective-permute-start
  136.5 25.9 %collective-permute-start.1 = (bf16[4,1,240,512]{3,2,1,0:T(8,128)(2,1)S(1)}, bf16[4,1,240,512]{3,2,1,0:T(8,128)(2,1)S(1)}, u32[]{:S(2)}, u32[]{:S(2)}) collective-permute-start(bf16[4,1,240,512]{3,2,1,0:T(8,128)(2,1)S(1)} %get-tuple-element.44), channel_id=1, source_target_pairs={{0,1},{1,2},{2,3},{3,4},{4,5},{5,6},{6,7},{7,8},{8,9},{9,10},{10,1... | collective-permute-start | bytes 2949128 | tf_op jit(solution)/shard_map/ppermute | solution.py:26
  140.2 26.6 %collective-permute-start.2 = (bf16[4,1,240,512]{3,2,1,0:T(8,128)(2,1)S(1)}, bf16[4,1,240,512]{3,2,1,0:T(8,128)(2,1)S(1)}, u32[]{:S(2)}, u32[]{:S(2)}) collective-permute-start(bf16[4,1,240,512]{3,2,1,0:T(8,128)(2,1)S(1)} %get-tuple-element.45), channel_id=1, source_target_pairs={{1,0},{2,1},{3,2},{4,3},{5,4},{6,5},{7,6},{8,7},{9,8},{10,9},{11,1... | collective-permute-start | bytes 2949128 | tf_op jit(solution)/shard_map/ppermute | solution.py:28
  176.0 2.1 copy-start.13
  197.7 2.5 copy-start.2
  197.7 2.5 copy-start.24
  200.2 132.1 %copy-start.25 = (f32[512]{0:T(512)S(1)}, f32[512]{0:T(512)}, u32[]{:S(2)}) copy-start(f32[512]{0:T(512)} %param.18) | copy-start | bytes 6148
  200.2 132.1 %copy-start.26 = (f32[512]{0:T(512)S(1)}, f32[512]{0:T(512)}, u32[]{:S(2)}) copy-start(f32[512]{0:T(512)} %param.17) | copy-start | bytes 6148
  200.6 132.8 %copy-start.3 = (bf16[2,2,240,512]{3,2,1,0:T(8,128)(2,1)}, bf16[2,2,240,512]{3,2,1,0:T(8,128)(2,1)S(1)}, u32[]{:S(2)}) copy-start(bf16[2,2,240,512]{3,2,1,0:T(8,128)(2,1)S(1)} %get-tuple-element.6) | copy-start | bytes 2949124
  332.7 2.4 copy-start.22
  335.1 184.7 %copy-start.23 = (bf16[2,2,240,512]{3,2,1,0:T(8,128)(2,1)S(1)}, bf16[2,2,240,512]{3,2,1,0:T(8,128)(2,1)}, u32[]{:S(2)}) copy-start(bf16[2,2,240,512]{3,2,1,0:T(8,128)(2,1)} %copy-done.22) | copy-start | bytes 2949124
  336.6 48.0 %collective-permute-start.3 = (bf16[2,2,2,240,512]{4,3,2,1,0:T(8,128)(2,1)}, bf16[2,2,2,240,512]{4,3,2,1,0:T(8,128)(2,1)}, u32[]{:S(2)}, u32[]{:S(2)}) collective-permute-start(bf16[2,2,2,240,512]{4,3,2,1,0:T(8,128)(2,1)} %pad_maximum_fusion.10), channel_id=1, source_target_pairs={{0,4},{1,5},{2,6},{3,7},{4,8},{5,9},{6,10},{7,11},{8,12},{9,13},{1... | collective-permute-start | bytes 5898248 | tf_op jit(solution)/shard_map/ppermute | solution.py:15
  340.4 86.0 %collective-permute-start.4 = (bf16[2,2,2,240,512]{4,3,2,1,0:T(8,128)(2,1)}, bf16[2,2,2,240,512]{4,3,2,1,0:T(8,128)(2,1)}, u32[]{:S(2)}, u32[]{:S(2)}) collective-permute-start(bf16[2,2,2,240,512]{4,3,2,1,0:T(8,128)(2,1)} %pad_maximum_fusion.10), channel_id=1, source_target_pairs={{0,3},{1,4},{2,5},{3,6},{4,7},{5,8},{6,9},{7,10},{8,11},{9,12},{10... | collective-permute-start | bytes 5898248 | tf_op jit(solution)/shard_map/ppermute | solution.py:15
  343.6 172.8 %collective-permute-start.5 = (bf16[2,2,2,240,512]{4,3,2,1,0:T(8,128)(2,1)}, bf16[2,2,2,240,512]{4,3,2,1,0:T(8,128)(2,1)}, u32[]{:S(2)}, u32[]{:S(2)}) collective-permute-start(bf16[2,2,2,240,512]{4,3,2,1,0:T(8,128)(2,1)} %pad_maximum_fusion.10), channel_id=1, source_target_pairs={{0,2},{1,3},{2,4},{3,5},{4,6},{5,7},{6,8},{7,9},{8,10},{9,11},{10,... | collective-permute-start | bytes 5898248 | tf_op jit(solution)/shard_map/ppermute | solution.py:15
  348.2 179.4 %collective-permute-start.6 = (bf16[2,2,2,240,512]{4,3,2,1,0:T(8,128)(2,1)}, bf16[2,2,2,240,512]{4,3,2,1,0:T(8,128)(2,1)}, u32[]{:S(2)}, u32[]{:S(2)}) collective-permute-start(bf16[2,2,2,240,512]{4,3,2,1,0:T(8,128)(2,1)} %pad_maximum_fusion.10), channel_id=1, source_target_pairs={{0,1},{1,2},{2,3},{3,4},{4,5},{5,6},{6,7},{7,8},{8,9},{9,10},{10,1... | collective-permute-start | bytes 5898248 | tf_op jit(solution)/shard_map/ppermute | solution.py:15
  351.2 178.2 %collective-permute-start.7 = (bf16[2,2,2,240,512]{4,3,2,1,0:T(8,128)(2,1)}, bf16[2,2,2,240,512]{4,3,2,1,0:T(8,128)(2,1)}, u32[]{:S(2)}, u32[]{:S(2)}) collective-permute-start(bf16[2,2,2,240,512]{4,3,2,1,0:T(8,128)(2,1)} %pad_maximum_fusion.10), channel_id=1, source_target_pairs={{1,0},{2,1},{3,2},{4,3},{5,4},{6,5},{7,6},{8,7},{9,8},{10,9},{11,1... | collective-permute-start | bytes 5898248 | tf_op jit(solution)/shard_map/ppermute | solution.py:15
  384.6 146.5 %collective-permute-start.8 = (bf16[2,2,2,240,512]{4,3,2,1,0:T(8,128)(2,1)}, bf16[2,2,2,240,512]{4,3,2,1,0:T(8,128)(2,1)}, u32[]{:S(2)}, u32[]{:S(2)}) collective-permute-start(bf16[2,2,2,240,512]{4,3,2,1,0:T(8,128)(2,1)} %pad_maximum_fusion.10), channel_id=1, source_target_pairs={{2,0},{3,1},{4,2},{5,3},{6,4},{7,5},{8,6},{9,7},{10,8},{11,9},{12,... | collective-permute-start | bytes 5898248 | tf_op jit(solution)/shard_map/ppermute | solution.py:15
  426.5 133.6 %collective-permute-start.9 = (bf16[2,2,2,240,512]{4,3,2,1,0:T(8,128)(2,1)}, bf16[2,2,2,240,512]{4,3,2,1,0:T(8,128)(2,1)}, u32[]{:S(2)}, u32[]{:S(2)}) collective-permute-start(bf16[2,2,2,240,512]{4,3,2,1,0:T(8,128)(2,1)} %pad_maximum_fusion.10), channel_id=1, source_target_pairs={{3,0},{4,1},{5,2},{6,3},{7,4},{8,5},{9,6},{10,7},{11,8},{12,9},{13... | collective-permute-start | bytes 5898248 | tf_op jit(solution)/shard_map/ppermute | solution.py:15
  516.5 125.7 %collective-permute-start.10 = (bf16[2,2,2,240,512]{4,3,2,1,0:T(8,128)(2,1)}, bf16[2,2,2,240,512]{4,3,2,1,0:T(8,128)(2,1)}, u32[]{:S(2)}, u32[]{:S(2)}) collective-permute-start(bf16[2,2,2,240,512]{4,3,2,1,0:T(8,128)(2,1)} %pad_maximum_fusion.10), channel_id=1, source_target_pairs={{4,0},{5,1},{6,2},{7,3},{8,4},{9,5},{10,6},{11,7},{12,8},{13,9},{1... | collective-permute-start | bytes 5898248 | tf_op jit(solution)/shard_map/ppermute | solution.py:15
  667.9 11.1 %copy-start.4 = (bf16[2,2,240,512]{3,2,1,0:T(8,128)(2,1)S(1)}, bf16[2,2,240,512]{3,2,1,0:T(8,128)(2,1)}, u32[]{:S(2)}) copy-start(bf16[2,2,240,512]{3,2,1,0:T(8,128)(2,1)} %copy-done.3) | copy-start | bytes 2949124
  667.9 11.1 %copy-start.27 = (bf16[512,512]{1,0:T(8,128)(2,1)S(1)}, bf16[512,512]{1,0:T(8,128)(2,1)}, u32[]{:S(2)}) copy-start(bf16[512,512]{1,0:T(8,128)(2,1)} %param.22) | copy-start | bytes 1572868
  667.9 11.1 %copy-start.28 = (f32[512]{0:T(512)S(1)}, f32[512]{0:T(512)}, u32[]{:S(2)}) copy-start(f32[512]{0:T(512)} %param.23) | copy-start | bytes 6148
  667.9 12.7 %copy-start.1 = (bf16[512,512]{1,0:T(8,128)(2,1)S(1)}, bf16[512,512]{1,0:T(8,128)(2,1)}, u32[]{:S(2)}) copy-start(bf16[512,512]{1,0:T(8,128)(2,1)} %param.20) | copy-start | bytes 1572868
  (16 other events, 25.9 us)
where the time goes:
time: 682 us; the launch traced here: 681 us
  blocking collectives  257 us (38%)
  waiting for transfers between devices  195 us (29%)
  starting transfers between devices  121 us (18%)
  matrix products  43.8 us (6%)
  local copies, waits for them, and re-layouts  40.4 us (6%)
  other arithmetic  22.8 us (3%)
    ppermute x9, waiting for transfers between devices, from_behind(): return lax.ppermute(array, axis, pairs)  180 us
    psum x2, blocking collectives, group_norm(): mean = lax.psum(local_sum, ('tm', 'rows')) / count  130 us
    psum x2, blocking collectives, group_norm(): lax.psum(jnp.sum(centered * centered, axis=(0, 1, 2, 4)), ('tm', 'rows'))  127 us
    ppermute x9, starting transfers between devices, from_behind(): return lax.ppermute(array, axis, pairs)  115 us
    unnamed x65, local copies, waits for them, and re-layouts  17.3 us
    dot_general x9, matrix products, conv_taps(): jnp.dot(stacked.reshape(-1, 3 * chans), weight[step_t, step_h].reshape(3...  15.9 us
  transfers between devices with their start and end apart: 11, of which 7 were waited for; matrix products, arithmetic and copies ran while one was open for 4% of the time, Pallas kernels for 0%

commit v1 on v0

--- a/solution.py
+++ b/solution.py
@@ -38,7 +38,12 @@
     local_sum = jnp.sum(grouped, axis=(0, 1, 2, 4))
     mean = lax.psum(local_sum, ("tm", "rows")) / count
     centered = grouped - mean[:, None]
-    spread = lax.psum(jnp.sum(centered * centered, axis=(0, 1, 2, 4)), ("tm", "rows")) / count
+    spread = (
+        jnp.sum(
+            lax.all_gather(jnp.sum(centered * centered, axis=(0, 1, 2, 4)), ("tm", "rows")), axis=0
+        )
+        / count
+    )
     normed = centered * lax.rsqrt(spread + EPS)[:, None]
     return normed.reshape(values.shape) * gain + shift
 

time: 682 us -> 683 us (level)
    unnamed x0 -> x2, blocking collectives: none -> 127 us
    psum x2 -> x0, blocking collectives: 127 us -> none  [group_norm(): lax.psum(jnp.sum(centered * centered, axis=(0, 1, 2, 4)), ('tm', 'rows'))]
    unnamed x65 -> x71, local copies, waits for them, and re-layouts: 17.3 us -> 17.4 us
where the time goes in v1:
time: 683 us; the launch traced here: 682 us
  blocking collectives  257 us (38%)
  waiting for transfers between devices  195 us (29%)
  starting transfers between devices  121 us (18%)
  matrix products  46.7 us (7%)
  local copies, waits for them, and re-layouts  38.9 us (6%)
  other arithmetic  22.4 us (3%)
    ppermute x9, waiting for transfers between devices, from_behind(): return lax.ppermute(array, axis, pairs)  180 us
    psum x2, blocking collectives, group_norm(): mean = lax.psum(local_sum, ('tm', 'rows')) / count  130 us
    unnamed x2, blocking collectives  127 us
    ppermute x9, starting transfers between devices, from_behind(): return lax.ppermute(array, axis, pairs)  115 us
    dot_general x9, matrix products, conv_taps(): jnp.dot(stacked.reshape(-1, 3 * chans), weight[step_t, step_h].reshape(3...  18.8 us
    unnamed x71, local copies, waits for them, and re-layouts  17.4 us
  transfers between devices with their start and end apart: 11, of which 7 were waited for; matrix products, arithmetic and copies ran while one was open for 4% of the time, Pallas kernels for 0%

profile of v1, /device:TPU:54, one launch (start us, length us, event | category | flops | bytes accessed | tf_op | source)
XLA Modules:
  0.0 681.6 jit_solution(11770985791621889881)
XLA Ops:
  1.7 63.7 %psum.14 = f32[32]{0:T(128)S(1)} all-reduce(f32[32]{0:T(128)S(1)} %reduce_sum.75), channel_id=1, replica_groups=mesh['tm'=2,'rows'=64] {'tm','rows'}, use_global_device_ids=true, to_apply=%region_2.0 | all-reduce | flops 32 | bytes 256 | tf_op jit(solution)/shard_map/psum | solution.py:39
  67.6 63.1 %all-reduce.1 = f32[4096]{0:T(1024)S(1)} all-reduce(f32[4096]{0:T(1024)S(1)} %dynamic-update-slice), channel_id=2, replica_groups=mesh['tm'=2,'rows'=64] {'tm','rows'}, use_global_device_ids=true, to_apply=%add.1 | all-reduce | flops 4096 | bytes 32768
  136.5 3.7 collective-permute-start.1
  142.5 9.3 %fusion.44 = (bf16[1,1,3,512,512]{4,3,2,1,0:T(8,128)(2,1)S(1)}, bf16[1,1,3,512,512]{4,3,2,1,0:T(8,128)(2,1)}, bf16[1,1,3,512,512]{4,3,2,1,0:T(8,128)(2,1)}, bf16...) fusion(bf16[3,3,3,512,512]{4,3,2,1,0:T(8,128)(2,1)} %param.15), kind=kLoop, calls=%fused_computation.89 | loop fusion | bytes 28311552 | tf_op jit(solution)/shard_map/slice | solution.py:62
  151.8 10.6 %collective-permute-done.1 = bf16[4,1,240,512]{3,2,1,0:T(8,128)(2,1)S(1)} collective-permute-done((bf16[4,1,240,512]{3,2,1,0:T(8,128)(2,1)S(1)}, bf16[4,1,240,512]{3,2,1,0:T(8,128)(2,1)S(1)}, u32[]{:S(2)}, u32[]{:S(2)}) %collective-permute-start.1) | collective-permute-done | bytes 983072 | tf_op jit(solution)/shard_map/ppermute | solution.py:26
  162.4 4.4 collective-permute-done.2
  168.9 4.5 fusion.45
  191.7 3.2 fusion.49
  201.4 66.4 %psum.15 = f32[32]{0:T(128)S(1)} all-reduce(f32[32]{0:T(128)S(1)} %reduce_sum.100), channel_id=1, replica_groups=mesh['tm'=2,'rows'=64] {'tm','rows'}, use_global_device_ids=true, to_apply=%region_8.9 | all-reduce | flops 32 | bytes 256 | tf_op jit(solution)/shard_map/psum | solution.py:39
  268.9 64.2 %all-reduce.2 = f32[4096]{0:T(1024)S(1)} all-reduce(f32[4096]{0:T(1024)S(1)} %dynamic-update-slice.1), channel_id=3, replica_groups=mesh['tm'=2,'rows'=64] {'tm','rows'}, use_global_device_ids=true, to_apply=%add.2 | all-reduce | flops 4096 | bytes 32768
  337.7 3.8 collective-permute-start.3
  341.5 3.3 collective-permute-start.4
  344.8 4.5 collective-permute-start.5
  349.3 3.0 collective-permute-start.6
  355.1 30.5 %collective-permute-done.3 = bf16[2,2,2,240,512]{4,3,2,1,0:T(8,128)(2,1)} collective-permute-done((bf16[2,2,2,240,512]{4,3,2,1,0:T(8,128)(2,1)}, bf16[2,2,2,240,512]{4,3,2,1,0:T(8,128)(2,1)}, u32[]{:S(2)}, u32[]{:S(2)}) %collective-permute-start.3) | collective-permute-done | bytes 1966112 | tf_op jit(solution)/shard_map/ppermute | solution.py:15
  388.3 39.4 %collective-permute-done.4 = bf16[2,2,2,240,512]{4,3,2,1,0:T(8,128)(2,1)} collective-permute-done((bf16[2,2,2,240,512]{4,3,2,1,0:T(8,128)(2,1)}, bf16[2,2,2,240,512]{4,3,2,1,0:T(8,128)(2,1)}, u32[]{:S(2)}, u32[]{:S(2)}) %collective-permute-start.4) | collective-permute-done | bytes 1966112 | tf_op jit(solution)/shard_map/ppermute | solution.py:15
  427.6 90.0 %collective-permute-start.9 = (bf16[2,2,2,240,512]{4,3,2,1,0:T(8,128)(2,1)}, bf16[2,2,2,240,512]{4,3,2,1,0:T(8,128)(2,1)}, u32[]{:S(2)}, u32[]{:S(2)}) collective-permute-start(bf16[2,2,2,240,512]{4,3,2,1,0:T(8,128)(2,1)} %pad_maximum_fusion.10), channel_id=1, source_target_pairs={{3,0},{4,1},{5,2},{6,3},{7,4},{8,5},{9,6},{10,7},{11,8},{12,9},{13... | collective-permute-start | bytes 5898248 | tf_op jit(solution)/shard_map/ppermute | solution.py:15
  517.7 3.1 collective-permute-start.10
  534.0 27.2 %collective-permute-done.9 = bf16[2,2,2,240,512]{4,3,2,1,0:T(8,128)(2,1)} collective-permute-done((bf16[2,2,2,240,512]{4,3,2,1,0:T(8,128)(2,1)}, bf16[2,2,2,240,512]{4,3,2,1,0:T(8,128)(2,1)}, u32[]{:S(2)}, u32[]{:S(2)}) %collective-permute-start.9) | collective-permute-done | bytes 1966112 | tf_op jit(solution)/shard_map/ppermute | solution.py:15
  562.9 80.4 %collective-permute-done.10 = bf16[2,2,2,240,512]{4,3,2,1,0:T(8,128)(2,1)} collective-permute-done((bf16[2,2,2,240,512]{4,3,2,1,0:T(8,128)(2,1)}, bf16[2,2,2,240,512]{4,3,2,1,0:T(8,128)(2,1)}, u32[]{:S(2)}, u32[]{:S(2)}) %collective-permute-start.10) | collective-permute-done | bytes 1966112 | tf_op jit(solution)/shard_map/ppermute | solution.py:15
  645.0 4.3 fusion.43
  649.3 10.1 %fusion = (f32[2,480]{1,0:T(2,128)S(1)}, f32[2,480,4320]{2,1,0:T(8,128)}) fusion(pred[4320]{0:T(1024)(128)(4,1)S(1)} %broadcast_in_dim.35, bf16[2,480,512]{2,1,0:T(8,128)(2,1)} %bitcast.89, bf16[2,4320,512]{2,1,0:T(8,128)(2,1)S(1)} %bitcast.63), kind=kOutput, calls=%fused_computation.2 | convolution fusion | flops 4259173376 | bytes 26427360 | tf_op jit(solution)/shard_map/fqc,fkc->fqk/dot_general | solution.py:122
  659.4 9.5 %fusion.1 = f32[2,480]{1,0:T(2,128)S(1)} fusion(f32[2,480,4320]{2,1,0:T(8,128)} %get-tuple-element.50, f32[2,480]{1,0:T(2,128)S(1)} %get-tuple-element.49, pred[4320]{0:T(1024)(128)(4,1)S(1)} %broadcast_in_dim.35), kind=kLoop, calls=%fused_computation.3 | loop fusion | flops 16587840 | bytes 16600800 | tf_op jit(solution)/shard_map/reduce_sum | solution.py:126
  668.9 11.0 %divide_convert_fusion = bf16[2,480,512]{2,1,0:T(8,128)(2,1)S(1)} fusion(bf16[2,4320,512]{2,1,0:T(8,128)(2,1)} %bitcast.62, f32[2,480,4320]{2,1,0:T(8,128)} %get-tuple-element.50, f32[2,480]{1,0:T(2,128)S(1)} %get-tuple-element.49, pred[4320]{0:T(1024)(128)(4,1)S(1)} %broadcast_in_dim.35, f32[2,480]{1,0:T(2,128)S(1)} %fusion.1), kind=kOutput, calls=%fused_computation.62 | convolution fusion | flops 4264304640 | bytes 26431200 | tf_op jit(solution)/shard_map/fqk,fkc->fqc/dot_general | solution.py:127
  (139 shorter events, 67.7 us)
Async XLA Ops:
  0.0 333.8 %copy-start = (bf16[512,512]{1,0:T(8,128)(2,1)S(1)}, bf16[512,512]{1,0:T(8,128)(2,1)}, u32[]{:S(2)}) copy-start(bf16[512,512]{1,0:T(8,128)(2,1)} %param.20) | copy-start | bytes 1572868
  0.0 130.9 %copy-start.2 = (bf16[2,2,240,512]{3,2,1,0:T(8,128)(2,1)S(1)}, bf16[2,2,240,512]{3,2,1,0:T(8,128)(2,1)}, u32[]{:S(2)}) copy-start(bf16[2,2,240,512]{3,2,1,0:T(8,128)(2,1)} %param.12) | copy-start | bytes 2949124
  132.3 3.9 collective-permute-start
  136.5 25.9 %collective-permute-start.1 = (bf16[4,1,240,512]{3,2,1,0:T(8,128)(2,1)S(1)}, bf16[4,1,240,512]{3,2,1,0:T(8,128)(2,1)S(1)}, u32[]{:S(2)}, u32[]{:S(2)}) collective-permute-start(bf16[4,1,240,512]{3,2,1,0:T(8,128)(2,1)S(1)} %get-tuple-element.44), channel_id=1, source_target_pairs={{0,1},{1,2},{2,3},{3,4},{4,5},{5,6},{6,7},{7,8},{8,9},{9,10},{10,1... | collective-permute-start | bytes 2949128 | tf_op jit(solution)/shard_map/ppermute | solution.py:26
  140.1 26.7 %collective-permute-start.2 = (bf16[4,1,240,512]{3,2,1,0:T(8,128)(2,1)S(1)}, bf16[4,1,240,512]{3,2,1,0:T(8,128)(2,1)S(1)}, u32[]{:S(2)}, u32[]{:S(2)}) collective-permute-start(bf16[4,1,240,512]{3,2,1,0:T(8,128)(2,1)S(1)} %get-tuple-element.45), channel_id=1, source_target_pairs={{1,0},{2,1},{3,2},{4,3},{5,4},{6,5},{7,6},{8,7},{9,8},{10,9},{11,1... | collective-permute-start | bytes 2949128 | tf_op jit(solution)/shard_map/ppermute | solution.py:28
  183.0 3.0 copy-start.19
  191.7 3.2 copy-start.17
  198.3 2.5 copy-start.25
  200.8 132.6 %copy-start.26 = (f32[512]{0:T(512)S(1)}, f32[512]{0:T(512)}, u32[]{:S(2)}) copy-start(f32[512]{0:T(512)} %param.18) | copy-start | bytes 6148
  200.8 132.6 %copy-start.27 = (f32[512]{0:T(512)S(1)}, f32[512]{0:T(512)}, u32[]{:S(2)}) copy-start(f32[512]{0:T(512)} %param.17) | copy-start | bytes 6148
  201.2 133.2 %copy-start.3 = (bf16[2,2,240,512]{3,2,1,0:T(8,128)(2,1)}, bf16[2,2,240,512]{3,2,1,0:T(8,128)(2,1)S(1)}, u32[]{:S(2)}) copy-start(bf16[2,2,240,512]{3,2,1,0:T(8,128)(2,1)S(1)} %get-tuple-element.6) | copy-start | bytes 2949124
  336.2 184.8 %copy-start.24 = (bf16[2,2,240,512]{3,2,1,0:T(8,128)(2,1)S(1)}, bf16[2,2,240,512]{3,2,1,0:T(8,128)(2,1)}, u32[]{:S(2)}) copy-start(bf16[2,2,240,512]{3,2,1,0:T(8,128)(2,1)} %copy-done.23) | copy-start | bytes 2949124
  337.7 48.0 %collective-permute-start.3 = (bf16[2,2,2,240,512]{4,3,2,1,0:T(8,128)(2,1)}, bf16[2,2,2,240,512]{4,3,2,1,0:T(8,128)(2,1)}, u32[]{:S(2)}, u32[]{:S(2)}) collective-permute-start(bf16[2,2,2,240,512]{4,3,2,1,0:T(8,128)(2,1)} %pad_maximum_fusion.10), channel_id=1, source_target_pairs={{0,4},{1,5},{2,6},{3,7},{4,8},{5,9},{6,10},{7,11},{8,12},{9,13},{1... | collective-permute-start | bytes 5898248 | tf_op jit(solution)/shard_map/ppermute | solution.py:15
  341.5 86.1 %collective-permute-start.4 = (bf16[2,2,2,240,512]{4,3,2,1,0:T(8,128)(2,1)}, bf16[2,2,2,240,512]{4,3,2,1,0:T(8,128)(2,1)}, u32[]{:S(2)}, u32[]{:S(2)}) collective-permute-start(bf16[2,2,2,240,512]{4,3,2,1,0:T(8,128)(2,1)} %pad_maximum_fusion.10), channel_id=1, source_target_pairs={{0,3},{1,4},{2,5},{3,6},{4,7},{5,8},{6,9},{7,10},{8,11},{9,12},{10... | collective-permute-start | bytes 5898248 | tf_op jit(solution)/shard_map/ppermute | solution.py:15
  344.8 172.9 %collective-permute-start.5 = (bf16[2,2,2,240,512]{4,3,2,1,0:T(8,128)(2,1)}, bf16[2,2,2,240,512]{4,3,2,1,0:T(8,128)(2,1)}, u32[]{:S(2)}, u32[]{:S(2)}) collective-permute-start(bf16[2,2,2,240,512]{4,3,2,1,0:T(8,128)(2,1)} %pad_maximum_fusion.10), channel_id=1, source_target_pairs={{0,2},{1,3},{2,4},{3,5},{4,6},{5,7},{6,8},{7,9},{8,10},{9,11},{10,... | collective-permute-start | bytes 5898248 | tf_op jit(solution)/shard_map/ppermute | solution.py:15
  349.3 179.5 %collective-permute-start.6 = (bf16[2,2,2,240,512]{4,3,2,1,0:T(8,128)(2,1)}, bf16[2,2,2,240,512]{4,3,2,1,0:T(8,128)(2,1)}, u32[]{:S(2)}, u32[]{:S(2)}) collective-permute-start(bf16[2,2,2,240,512]{4,3,2,1,0:T(8,128)(2,1)} %pad_maximum_fusion.10), channel_id=1, source_target_pairs={{0,1},{1,2},{2,3},{3,4},{4,5},{5,6},{6,7},{7,8},{8,9},{9,10},{10,1... | collective-permute-start | bytes 5898248 | tf_op jit(solution)/shard_map/ppermute | solution.py:15
  352.3 178.3 %collective-permute-start.7 = (bf16[2,2,2,240,512]{4,3,2,1,0:T(8,128)(2,1)}, bf16[2,2,2,240,512]{4,3,2,1,0:T(8,128)(2,1)}, u32[]{:S(2)}, u32[]{:S(2)}) collective-permute-start(bf16[2,2,2,240,512]{4,3,2,1,0:T(8,128)(2,1)} %pad_maximum_fusion.10), channel_id=1, source_target_pairs={{1,0},{2,1},{3,2},{4,3},{5,4},{6,5},{7,6},{8,7},{9,8},{10,9},{11,1... | collective-permute-start | bytes 5898248 | tf_op jit(solution)/shard_map/ppermute | solution.py:15
  385.7 146.6 %collective-permute-start.8 = (bf16[2,2,2,240,512]{4,3,2,1,0:T(8,128)(2,1)}, bf16[2,2,2,240,512]{4,3,2,1,0:T(8,128)(2,1)}, u32[]{:S(2)}, u32[]{:S(2)}) collective-permute-start(bf16[2,2,2,240,512]{4,3,2,1,0:T(8,128)(2,1)} %pad_maximum_fusion.10), channel_id=1, source_target_pairs={{2,0},{3,1},{4,2},{5,3},{6,4},{7,5},{8,6},{9,7},{10,8},{11,9},{12,... | collective-permute-start | bytes 5898248 | tf_op jit(solution)/shard_map/ppermute | solution.py:15
  427.6 133.6 %collective-permute-start.9 = (bf16[2,2,2,240,512]{4,3,2,1,0:T(8,128)(2,1)}, bf16[2,2,2,240,512]{4,3,2,1,0:T(8,128)(2,1)}, u32[]{:S(2)}, u32[]{:S(2)}) collective-permute-start(bf16[2,2,2,240,512]{4,3,2,1,0:T(8,128)(2,1)} %pad_maximum_fusion.10), channel_id=1, source_target_pairs={{3,0},{4,1},{5,2},{6,3},{7,4},{8,5},{9,6},{10,7},{11,8},{12,9},{13... | collective-permute-start | bytes 5898248 | tf_op jit(solution)/shard_map/ppermute | solution.py:15
  517.7 125.6 %collective-permute-start.10 = (bf16[2,2,2,240,512]{4,3,2,1,0:T(8,128)(2,1)}, bf16[2,2,2,240,512]{4,3,2,1,0:T(8,128)(2,1)}, u32[]{:S(2)}, u32[]{:S(2)}) collective-permute-start(bf16[2,2,2,240,512]{4,3,2,1,0:T(8,128)(2,1)} %pad_maximum_fusion.10), channel_id=1, source_target_pairs={{4,0},{5,1},{6,2},{7,3},{8,4},{9,5},{10,6},{11,7},{12,8},{13,9},{1... | collective-permute-start | bytes 5898248 | tf_op jit(solution)/shard_map/ppermute | solution.py:15
  668.9 11.1 %copy-start.4 = (bf16[2,2,240,512]{3,2,1,0:T(8,128)(2,1)S(1)}, bf16[2,2,240,512]{3,2,1,0:T(8,128)(2,1)}, u32[]{:S(2)}) copy-start(bf16[2,2,240,512]{3,2,1,0:T(8,128)(2,1)} %copy-done.3) | copy-start | bytes 2949124
  668.9 11.1 %copy-start.28 = (bf16[512,512]{1,0:T(8,128)(2,1)S(1)}, bf16[512,512]{1,0:T(8,128)(2,1)}, u32[]{:S(2)}) copy-start(bf16[512,512]{1,0:T(8,128)(2,1)} %param.22) | copy-start | bytes 1572868
  668.9 11.1 %copy-start.29 = (f32[512]{0:T(512)S(1)}, f32[512]{0:T(512)}, u32[]{:S(2)}) copy-start(f32[512]{0:T(512)} %param.23) | copy-start | bytes 6148
  668.9 12.7 %copy-start.1 = (bf16[512,512]{1,0:T(8,128)(2,1)S(1)}, bf16[512,512]{1,0:T(8,128)(2,1)}, u32[]{:S(2)}) copy-start(bf16[512,512]{1,0:T(8,128)(2,1)} %param.20) | copy-start | bytes 1572868
  (17 other events, 29.0 us)
